TPU v7x, 32 devices: a whole 2x2x4 slice. The times are simulated.
32 devices in a mesh: dp: 8 (over y, x, core), tensor: 4 (over z).
Axes of the slice: x: 2, y: 2, z: 4, core: 2. Of those that a mesh axis runs over, the one named last changes fastest.
Arguments:
- tokens: bfloat16 [16384, 768], P(('dp', 'tensor')), may hold values from -6 to 6
- cotangent: bfloat16 [16384, 768], P(('dp', 'tensor')), may hold values from -6 to 6
- deal: int32 [16384], P(('dp', 'tensor')), may hold values from 0 to 7, as said below
- lengths: int32 [8, 8], P('dp'), may hold values from 1 to 1024, 2048 in all within a row
- routes: int32 [16384, 2], P('dp'), may hold values from 0 to 11, all different within a row; in each aligned block of 2048 rows (0 to 2047, 2048 to 4095, ...) at most 512 rows name the same one
- gate_residual: float32 [16384, 12], P(('dp', 'tensor')), may hold values from -4 to 4
- w_qkv: bfloat16 [768, 3, 768], P('dp', None, 'tensor'), may hold values from -0.21875 to 0.21875
- w_out: bfloat16 [768, 768], P('dp', 'tensor'), may hold values from -1.25 to 1.25
- w_gate_up: bfloat16 [768, 8, 2, 2048], P('dp', None, None, 'tensor'), may hold values from -0.21875 to 0.21875
- w_down: bfloat16 [768, 8, 2048], P('dp', None, 'tensor'), may hold values from -0.25 to 0.25
- norm_gain_attn: float32 [768], replicated, may hold values from 0.1 to 1.9
- norm_gain_moe: float32 [768], replicated, may hold values from 0.1 to 1.9
- w_router: float32 [768, 12], replicated, may hold values from -0.15625 to 0.15625
- w_const: float32 [2, 768, 2], replicated, may hold values from -0.21875 to 0.21875
- v_const: float32 [2, 768], replicated, may hold values from -5 to 5
Outputs:
- output: bfloat16 [16384, 768], P(('dp', 'tensor'))
- grad_tokens: bfloat16 [16384, 768], P(('dp', 'tensor'))
- grad_residual: float32 [16384, 12], P(('dp', 'tensor'))
- grad_qkv: float32 [768, 3, 768], P('dp', None, 'tensor')
- grad_out: float32 [768, 768], P('dp', 'tensor')
- grad_gate_up: float32 [768, 8, 2, 2048], P('dp', None, None, 'tensor')
- grad_down: float32 [768, 8, 2048], P('dp', None, 'tensor')
- grad_gain_attn: float32 [768], replicated
- grad_gain_moe: float32 [768], replicated
- grad_router: float32 [768, 12], replicated
- grad_const: float32 [2, 768, 2], replicated
- grad_vconst: float32 [2, 768], replicated
Inputs may be any that keep to these rules, and one draw needn't show every extreme that they name: `deal`: every device deals exactly 64 of its tokens to each index of dp. Each row of a group's lengths sums to 2048; its largest is 1024. `routes`: A row names two different experts: 0 to 7 feed-forward, 8 zero, 9 copy, 10 and 11 constant. In the 2048 rows of one token group no expert is named by more than 512 rows, a bound that some block reaches.
All inputs are finite; a program needn't handle non-finite values.
Results may differ from a plain program's by a relative error of at most 0.02.
Values may be sent and summed in bfloat16 or wider, within the bound.
A program may use at most 256 MiB of HBM per device.

v0:
```python
import functools

import jax
import jax.numpy as jnp
import numpy as np
from jax import lax
from jax.experimental import pallas as pl
from jax.experimental.pallas import tpu as pltpu
from jax.sharding import PartitionSpec as P

D = 768
HEAD_DIM = 64
HEADS = 12
EXPERTS = 8
LONGEST = 1024
EPSILON = 1e-6
MASKED = -1e30
F32, BF16, I32 = jnp.float32, jnp.bfloat16, jnp.int32
NN = (((1,), (0,)), ((), ()))
NT = (((1,), (1,)), ((), ()))
TN = (((0,), (0,)), ((), ()))
SCORE_SCALE = HEAD_DIM**-0.5
LOG2E = 1.4426950408889634
TILE = 160
ROWS = 256
SPARE = 16
VMEM_CAP = 66_000_000


def mm(a, b, dims):
    return lax.dot_general(a, b, dims, preferred_element_type=F32)


def iota(shape, axis):
    return lax.broadcasted_iota(I32, shape, axis)


def pick(cond):
    return jnp.where(cond, 1.0, 0.0).astype(BF16)


def split2(v):
    high = v.astype(BF16)
    return high, (v - high.astype(F32)).astype(BF16)


def split3(v):
    high = v.astype(BF16)
    rest = v - high.astype(F32)
    mid = rest.astype(BF16)
    return high, mid, (rest - mid.astype(F32)).astype(BF16)


def vmem():
    return pl.BlockSpec(memory_space=pltpu.VMEM)


def smem():
    return pl.BlockSpec(memory_space=pltpu.SMEM)


def call(body, name, outs, operands, scalars=0, scratch=(), meet=None):
    return pl.pallas_call(
        body,
        name=name,
        out_shape=[jax.ShapeDtypeStruct(*o) for o in outs],
        in_specs=[smem()] * scalars + [vmem()] * (len(operands) - scalars),
        out_specs=[vmem()] * len(outs),
        scratch_shapes=list(scratch),
        compiler_params=pltpu.CompilerParams(
            vmem_limit_bytes=VMEM_CAP, collective_id=meet, has_side_effects=meet is not None
        ),
    )(*operands)


def deal_body(n_dp, deal_ref, tok_ref, cot_ref, routes_ref, xs_ref, gs_ref, pos_ref, slot_ref, cnt_ref):
    rows = tok_ref.shape[0]
    first, second = iota((rows, rows), 0), iota((rows, rows), 1)
    before = pick(first < second)
    deal = deal_ref[...]
    hit = iota((n_dp, rows), 0) == deal
    rank = mm(pick(hit), before, NN)
    rank = jnp.sum(jnp.where(hit, rank, 0.0), axis=0, keepdims=True).astype(I32)
    pos = deal * (rows // n_dp) + rank
    pos_ref[...] = pos
    place = pick(first == pos)
    xs_ref[...] = mm(place, tok_ref[...], NN).astype(BF16)
    gs_ref[...] = mm(place, cot_ref[...], NN).astype(BF16)
    expert = iota((EXPERTS, rows), 0)
    for j in range(routes_ref.shape[0]):
        route = routes_ref[j]
        named = (expert == route[0:1]) | (expert == route[1:2])
        ahead = mm(pick(named), before, NN).astype(I32)
        slot_ref[j] = jnp.where(named, ahead, -1)
        total = jnp.sum(jnp.where(named, 1.0, 0.0), axis=1, keepdims=True).astype(I32)
        cnt_ref[j] = jnp.broadcast_to(total, (EXPERTS, 128))


def restore_body(pos_ref, a_ref, b_ref, oa_ref, ob_ref):
    rows = a_ref.shape[0]
    place = pick(iota((rows, rows), 0) == pos_ref[...])
    oa_ref[...] = mm(place, a_ref[...], TN).astype(BF16)
    ob_ref[...] = mm(place, b_ref[...], TN).astype(BF16)


class Line:
    def __init__(self, size):
        self.size = size
        self.place = lax.axis_index("tensor")
        self.sent = {k: [] for k in range(size)}

    def each(self, body):
        for k in range(self.size):
            pl.when(self.place == k)(functools.partial(body, k))

    def enter(self):
        sem = pltpu.get_barrier_semaphore()

        def greet(k):
            near = [n for n in (k - 1, k + 1) if 0 <= n < self.size]
            for n in near:
                pl.semaphore_signal(sem, 1, device_id={"tensor": self.place + (n - k)}, device_id_type=pl.DeviceIdType.MESH)
            pl.semaphore_wait(sem, len(near))

        self.each(greet)

    def copy(self, hop, src, dst, sems):
        return pltpu.make_async_remote_copy(
            src_ref=src,
            dst_ref=dst,
            send_sem=sems[0],
            recv_sem=sems[1],
            device_id={"tensor": self.place + hop},
            device_id_type=pl.DeviceIdType.MESH,
        )

    def send(self, k, to, refs):
        self.copy(to - k, *refs()).start()
        self.sent[k].append((to - k, refs))

    def arrived(self, k, dst, sems):
        self.copy((k ^ 1) - k, dst, dst, sems).wait_recv()

    def leave(self):
        def drain(k):
            for hop, refs in self.sent[k]:
                self.copy(hop, *refs()).wait_send()

        self.each(drain)


class Peers:
    def __init__(self):
        self.d, self.t = lax.axis_index("dp"), lax.axis_index("tensor")
        self.sent = []

    def enter(self, targets):
        sem = pltpu.get_barrier_semaphore()
        for where in targets:
            pl.semaphore_signal(sem, 1, device_id=where, device_id_type=pl.DeviceIdType.MESH)
        pl.semaphore_wait(sem, len(targets))

    def copy(self, where, src, dst, sems):
        return pltpu.make_async_remote_copy(
            src_ref=src,
            dst_ref=dst,
            send_sem=sems[0],
            recv_sem=sems[1],
            device_id=where,
            device_id_type=pl.DeviceIdType.MESH,
        )

    def send(self, where, src, dst, sems):
        copy = self.copy(where, src, dst, sems)
        copy.start()
        self.sent.append(copy)

    def leave(self):
        for copy in self.sent:
            copy.wait_send()


def flip(index, bit):
    return index + bit * (1 - 2 * ((index // bit) % 2))


def around(index, count):
    return [(j, lax.rem(index + j, count), lax.rem(index + count - j, count)) for j in range(1, count)]


class Rows:
    def __init__(self, ref):
        self.ref = ref

    def __getitem__(self, at):
        columns = slice(None) if at is Ellipsis else at[1]
        value = self.ref[:, :, columns]
        return value.reshape(value.shape[0] * value.shape[1], value.shape[2])


def sum_events(size, k):
    events = []
    for dest in range(size):
        if dest >= k and dest > 0:
            events.append((0 if k == 0 else size - 1 - dest + k, 1, dest))
        if dest <= k and dest < size - 1:
            events.append((0 if k == size - 1 else dest + size - 1 - k, -1, dest))
    drop = [(t, w, d) for t, w, d in events if (k == 0 and w == 1 and d == 0) or (k == size - 1 and w == -1 and d == k)]
    return sorted((ev for ev in events if ev not in drop), key=lambda ev: (ev[0], ev[1], -ev[1] * ev[2]))


def turn(u):
    low = (iota((1, u.shape[1]), 1) % HEAD_DIM) < HEAD_DIM // 2
    half = HEAD_DIM // 2
    return jnp.where(low, pltpu.roll(u, u.shape[1] - half, 1), pltpu.roll(u, half, 1))


def wide(table):
    return jnp.concatenate([table] * (D // 128), axis=1)


def key_bias(start, block, first_row, base):
    window = LONGEST + block
    key = iota((window, block), 0) + first_row
    row = iota((1, block), 1) + (base + first_row)
    return jnp.where((key >= start) & (key <= row), 0.0, MASKED)


def router_part(route, o_ref, w_ref, x_ref, gain_ref, res_ref, wrc_ref, x1_ref, hp_ref, gt_ref):
    rows = o_ref.shape[0]
    x1 = x_ref[...].astype(F32) + mm(o_ref[...], w_ref[:, 3 * D : 4 * D], NT)
    x1_ref[...] = x1
    h = x1 * lax.rsqrt(jnp.mean(x1 * x1, axis=1, keepdims=True) + EPSILON) * gain_ref[...]
    h = h.astype(BF16)
    hp_ref[0:rows, :] = h
    high, mid, low = split3(wrc_ref[...])
    z = mm(low, h, NT) + mm(mid, h, NT) + mm(high, h, NT) + res_ref[...]
    expert = iota(z.shape, 0)
    named0, named1 = expert == route[0:1], expert == route[1:2]
    c0 = jnp.sum(jnp.where(named0, z, 0.0), axis=0, keepdims=True)
    c1 = jnp.sum(jnp.where(named1, z, 0.0), axis=0, keepdims=True)
    top = jnp.maximum(c0, c1)
    e0, e1 = jnp.exp(c0 - top), jnp.exp(c1 - top)
    g0, g1 = e0 / (e0 + e1), e1 / (e0 + e1)
    table = [g0, g1]
    for j in range(2):
        l0, l1 = z[12 + 2 * j : 13 + 2 * j], z[13 + 2 * j : 14 + 2 * j]
        top = jnp.maximum(l0, l1)
        m0, m1 = jnp.exp(l0 - top), jnp.exp(l1 - top)
        table += [m0 / (m0 + m1), m1 / (m0 + m1)]
    gt_ref[...] = jnp.concatenate(table + [jnp.zeros((2, rows), F32)], axis=0)
    gates = jnp.where(named0, g0, jnp.where(named1, g1, 0.0))
    gates = jnp.where(expert < EXPERTS, gates, 0.0)
    hp_ref[rows : rows + SPARE, :] = jnp.concatenate([gates, jnp.zeros((SPARE, D - rows), F32)], axis=1).astype(BF16)


def local_part(route, x1_ref, hp_ref, g_ref, gt_ref, v_ref, xl_ref, dhl_ref, sm_ref, gv_ref):
    rows = x1_ref.shape[0]
    h, g = hp_ref[0:rows, :], g_ref[...]
    hf, gf = h.astype(F32), g.astype(F32)
    low0 = gt_ref[0:1].astype(BF16).astype(F32)
    low1 = gt_ref[1:2].astype(BF16).astype(F32)

    def weight(e):
        return jnp.where(route[0:1] == e, low0, 0.0) + jnp.where(route[1:2] == e, low1, 0.0)

    copy, first, second = weight(EXPERTS + 1), weight(EXPERTS + 2), weight(EXPERTS + 3)
    m00, m01, m10, m11 = gt_ref[2:3], gt_ref[3:4], gt_ref[4:5], gt_ref[5:6]
    a = copy + first * m00 + second * m10
    b0, b1 = first * m01, second * m11
    table = jnp.concatenate([a, b0, b1, jnp.zeros((125, rows), F32)], axis=0).T
    ac, b0c, b1c = table[:, 0:1], table[:, 1:2], table[:, 2:3]
    v = v_ref[...]
    xl_ref[...] = x1_ref[...] + ac * hf + b0c * v[0:1] + b1c * v[1:2]
    dhl_ref[...] = ac * gf
    ones = jnp.ones((8, D), BF16)
    high, low = split2(hf * gf)
    gh = (mm(ones, high, NT) + mm(ones, low, NT))[0:1]
    vh, vm, vl = split3(v)
    gvs = mm(vl, g, NT) + mm(vm, g, NT) + mm(vh, g, NT)
    gv0, gv1 = gvs[0:1], gvs[1:2]
    zero = jnp.zeros((9, rows), F32)
    dl0 = first * m00 * m01 * (gh - gv0)
    dl1 = second * m10 * m11 * (gh - gv1)
    sm_ref[...] = jnp.concatenate(
        [zero, gh, m00 * gh + m01 * gv0, m10 * gh + m11 * gv1, dl0, -dl0, dl1, -dl1], axis=0
    )
    bh, bm, bl = split3(jnp.concatenate([b0, b1, jnp.zeros((6, rows), F32)], axis=0))
    gv_ref[...] = mm(bl, g, NN) + mm(bm, g, NN) + mm(bh, g, NN)


def rope_tables(lengths_ref, rates_ref, t, rows, cos_ref, sin_ref, start_ref):
    begins, total = [], jnp.int32(0)
    for i in range(lengths_ref.shape[0]):
        begins.append(total)
        total = total + lengths_ref[i]

    def opening(row):
        found = jnp.zeros_like(row)
        for begin in begins:
            found = jnp.where(begin <= row, jnp.maximum(found, begin), found)
        return found

    start_ref[...] = LONGEST - t * rows + opening(iota((1, rows), 1) + t * rows)
    sign = jnp.where(iota((1, 128), 1) % HEAD_DIM < HEAD_DIM // 2, -1.0, 1.0)
    step = 128

    def tile(i, _):
        at = pl.multiple_of(i * step, step)
        row = iota((step, 128), 0) + (at + (t - 2) * rows)
        angles = (row - opening(row)).astype(F32) * rates_ref[...]
        cos_ref[pl.ds(at, step), :] = jnp.cos(angles)
        sin_ref[pl.ds(at, step), :] = jnp.sin(angles) * sign
        return 0

    lax.fori_loop(0, cos_ref.shape[0] // step, tile, 0)


def opening_body(n_dp, size, lengths_ref, xs_ref, gs_ref, ws_ref, rates_ref,
                 x0_ref, g0_ref, w3_ref, x1_ref, x2_ref, cos_ref, sin_ref, start_ref,
                 wz_ref, sz, rz, sa, ra, sb, rb, s1, r1, s2, r2, s3, r3, sx, rx):
    rows = x0_ref.shape[0] * x0_ref.shape[1]
    line = Line(size)
    t = line.place
    last = size - 1

    def begin(k):
        if k < last:
            line.send(k, k + 1, lambda: (x0_ref, x1_ref, (sx.at[0], rx.at[0])))

    def second(k):
        if k > 0:
            line.arrived(k, x1_ref, (sx.at[0], rx.at[0]))
        else:
            x1_ref[...] = jnp.zeros_like(x1_ref)
        if 0 < k < last:
            line.send(k, k + 1, lambda: (x1_ref, x2_ref, (sx.at[1], rx.at[1])))

    def third(k):
        if k > 1:
            line.arrived(k, x2_ref, (sx.at[1], rx.at[1]))
        else:
            x2_ref[...] = jnp.zeros_like(x2_ref)

    net = Peers()
    d = net.d
    along, about = around(t, size), around(d, n_dp)
    net.enter([{"dp": to} for _, to, _ in about] + [{"tensor": to} for _, to, _ in along])
    for j, to, _ in along:
        net.send({"tensor": to}, ws_ref, wz_ref.at[t], (sz.at[j - 1], rz.at[j - 1]))
    for src_ref, dst_ref, ss, rr in ((xs_ref, x0_ref, sa, ra), (gs_ref, g0_ref, sb, rb)):
        for j, to, _ in about:
            net.send({"dp": to}, src_ref.at[to], dst_ref.at[d], (ss.at[j - 1], rr.at[j - 1]))
        dst_ref[d] = src_ref[d]
    wz_ref[t] = ws_ref[...]
    rope_tables(lengths_ref, rates_ref, t, rows, cos_ref, sin_ref, start_ref)

    def gathered(dst_ref, ss, rr):
        for j, _, source in about:
            held = dst_ref.at[source]
            net.copy({"dp": source}, held, held, (ss.at[j - 1], rr.at[j - 1])).wait_recv()

    gathered(x0_ref, sa, ra)
    line.each(begin)
    for j, _, source in along:
        held = wz_ref.at[source]
        net.copy({"tensor": source}, held, held, (sz.at[j - 1], rz.at[j - 1])).wait_recv()
    for c in range(4):
        w3_ref[d, :, c * D : (c + 1) * D] = jnp.concatenate([wz_ref[p, c] for p in range(size)], axis=1)
    pair, across = flip(d, 1), (flip(d, 2), flip(d, 4))
    halves = (slice(0, 2 * D), slice(2 * D, 4 * D))

    def pass_on(way, spot, half, sems):
        net.send({"dp": way}, w3_ref.at[spot, :, halves[half]], w3_ref.at[spot, :, halves[half]], sems)

    def passed(way, spot, half, sems):
        held = w3_ref.at[spot, :, halves[half]]
        net.copy({"dp": way}, held, held, sems).wait_recv()

    for half in range(2):
        pass_on(across[half], d, half, (s1.at[half], r1.at[half]))
    for half in range(2):
        near, far = across[half], across[1 - half]
        passed(near, near, half, (s1.at[half], r1.at[half]))
        for i, spot in enumerate((d, near)):
            pass_on(far, spot, half, (s2.at[half, i], r2.at[half, i]))
    line.each(second)
    beyond = flip(across[0], 4)
    for half in range(2):
        near, far = across[half], across[1 - half]
        for i, spot in enumerate((far, beyond)):
            passed(far, spot, half, (s2.at[half, i], r2.at[half, i]))
    core = lax.rem(d, 2)
    for i in range(n_dp // 2):
        spot = 2 * i + core
        net.send({"dp": pair}, w3_ref.at[spot], w3_ref.at[spot], (s3.at[i], r3.at[i]))
    for i in range(n_dp // 2):
        held = w3_ref.at[2 * i + 1 - core]
        net.copy({"dp": pair}, held, held, (s3.at[i], r3.at[i])).wait_recv()
    gathered(g0_ref, sb, rb)
    line.each(third)
    line.leave()
    net.leave()


def forward_body(fast, size, *refs):
    if fast:
        (x0_ref, g0_ref, w3_ref, x1_ref, x2_ref, cos_ref, sin_ref, start_ref), refs = refs[:8], refs[8:]
    else:
        (lengths_ref, rates_ref, x0_ref, g0_ref, w3_ref), refs = refs[:5], refs[5:]
    (gain_ref, gain2_ref, res_ref, wrc_ref, routes_ref, v8_ref), refs = refs[:6], refs[6:]
    if not fast:
        (x1_ref, x2_ref, cos_ref, sin_ref, start_ref), refs = refs[:5], refs[5:]
    (h_ref, q_ref, k_ref, v_ref, o_ref, lse_ref, xm_ref, hp_ref, gall_ref, gt_ref, xl_ref, dhl_ref, sm_ref, gv_ref,
     bias_ref, sx, rx, sgu, rgu, sgd, rgd, shu, rhu, shd, rhd) = refs
    rows = x0_ref.shape[0] * x0_ref.shape[1]
    step = 256
    line = Line(size)
    t = line.place
    last = size - 1
    w_ref, x_own, g_own = Rows(w3_ref), Rows(x0_ref), Rows(g0_ref)

    def begin(k):
        if k < last:
            if not fast:
                line.send(k, k + 1, lambda: (x0_ref, x1_ref, (sx.at[0], rx.at[0])))
            line.send(k, k + 1, lambda: (g0_ref, gall_ref.at[k], (sgu.at[0], rgu.at[0])))
        if k > 0:
            line.send(k, k - 1, lambda: (g0_ref, gall_ref.at[k], (sgd.at[0], rgd.at[0])))

    def first_rows(k):
        if k > 0:
            line.arrived(k, x1_ref, (sx.at[0], rx.at[0]))
        else:
            x1_ref[...] = jnp.zeros_like(x1_ref)
        if 0 < k < last:
            line.send(k, k + 1, lambda: (x1_ref, x2_ref, (sx.at[1], rx.at[1])))

    def second_rows(k):
        if k > 1:
            line.arrived(k, x2_ref, (sx.at[1], rx.at[1]))
        else:
            x2_ref[...] = jnp.zeros_like(x2_ref)

    def hop(k, far):
        up, down = k - far, k + far
        if up >= 0:
            line.arrived(k, gall_ref.at[up], (sgu.at[far - 1], rgu.at[far - 1]))
            if k < last:
                line.send(k, k + 1, lambda: (gall_ref.at[up], gall_ref.at[up], (sgu.at[far], rgu.at[far])))
        if down <= last:
            line.arrived(k, gall_ref.at[down], (sgd.at[far - 1], rgd.at[far - 1]))
            if k > 0:
                line.send(k, k - 1, lambda: (gall_ref.at[down], gall_ref.at[down], (sgd.at[far], rgd.at[far])))

    line.enter()
    line.each(begin)
    gall_ref[t] = g0_ref[...]
    if not fast:
        rope_tables(lengths_ref, rates_ref, t, rows, cos_ref, sin_ref, start_ref)
    gain = gain_ref[...]

    def part(x_ref, i):
        share = x_ref.shape[1]
        if share == rows:
            return x_ref[0, pl.ds(pl.multiple_of(i * step, step), step), :]
        return x_ref[pl.ds(i * (step // share), step // share)].reshape(step, D)

    def project_chunk(c, x_ref):
        def project(i, _):
            at = pl.multiple_of(i * step, step)
            x = part(x_ref, i).astype(F32)
            h = x * lax.rsqrt(jnp.mean(x * x, axis=1, keepdims=True) + EPSILON) * gain
            h = h.astype(BF16)
            to = pl.ds(pl.multiple_of(c * rows + i * step, step), step)
            h_ref[to, :] = h
            cos, sin = wide(cos_ref[to, :]), wide(sin_ref[to, :])
            k = mm(h, w_ref[:, D : 2 * D], NN)
            k_ref[to, :] = (k * cos + turn(k) * sin).astype(BF16)
            v_ref[to, :] = mm(h, w_ref[:, 2 * D : 3 * D], NN).astype(BF16)
            if c == 2:
                q = mm(h, w_ref[:, 0:D], NN)
                q_ref[pl.ds(at, step), :] = (q * cos + turn(q) * sin).astype(BF16)
            return 0

        lax.fori_loop(0, rows // step, project, 0)

    project_chunk(2, x0_ref)
    if not fast:
        line.each(first_rows)
    project_chunk(1, x1_ref)
    if not fast:
        line.each(second_rows)
    project_chunk(0, x2_ref)
    line.each(lambda k: hop(k, 1))

    block = step
    window = LONGEST + block
    lane = iota((1, 128), 1) // HEAD_DIM
    for rb in range(rows // block):
        first = rb * block
        bias_ref[...] = key_bias(start_ref[:, first : first + block], block, first, LONGEST)

        def pair(i, _, first=first):
            lanes = pl.ds(pl.multiple_of(i * 128, 128), 128)
            k = k_ref[first : first + window, lanes]
            vt = v_ref[first : first + window, lanes].T
            q = q_ref[first : first + block, lanes]
            parts = []
            for half in range(2):
                qm = jnp.where(lane == half, q, jnp.zeros_like(q))
                s = mm(k, qm, NT) * (SCORE_SCALE * LOG2E) + bias_ref[...]
                top = jnp.max(s, axis=0, keepdims=True)
                p = jnp.exp2(s - top)
                total = jnp.sum(p, axis=0, keepdims=True)
                out = mm(vt[half * HEAD_DIM : (half + 1) * HEAD_DIM], p.astype(BF16), NN)
                parts.append(out * (1.0 / total))
                lse_ref[pl.ds(i * 2 + half, 1), first : first + block] = top + jnp.log2(total)
            o_ref[first : first + block, lanes] = jnp.concatenate(parts, axis=0).T.astype(BF16)
            return 0

        lax.fori_loop(0, HEADS // 2, pair, 0)
        if rb == 0:
            line.each(lambda k: hop(k, 2))

    route = routes_ref[t]
    router_part(route, o_ref, w_ref, x_own, gain2_ref, res_ref, wrc_ref, xm_ref, hp_ref.at[t], gt_ref)

    def fifth(k):
        if k < last:
            line.send(k, k + 1, lambda: (hp_ref.at[k], hp_ref.at[k], (shu.at[0], rhu.at[0])))
        if k > 0:
            line.send(k, k - 1, lambda: (hp_ref.at[k], hp_ref.at[k], (shd.at[0], rhd.at[0])))

    line.each(fifth)
    local_part(route, xm_ref, hp_ref.at[t], g_own, gt_ref, v8_ref, xl_ref, dhl_ref, sm_ref, gv_ref)

    def sixth(k):
        for hop in range(2):
            up, down = k - 1 - hop, k + 1 + hop
            if up >= 0:
                line.arrived(k, hp_ref.at[up], (shu.at[hop], rhu.at[hop]))
                if k < last:
                    line.send(k, k + 1, lambda up=up, hop=hop: (hp_ref.at[up], hp_ref.at[up], (shu.at[hop + 1], rhu.at[hop + 1])))
            if down <= last:
                line.arrived(k, hp_ref.at[down], (shd.at[hop], rhd.at[hop]))
                if k > 0:
                    line.send(k, k - 1, lambda down=down, hop=hop: (hp_ref.at[down], hp_ref.at[down], (shd.at[hop + 1], rhd.at[hop + 1])))
        if k == last:
            line.arrived(k, hp_ref.at[0], (shu.at[2], rhu.at[2]))
            line.arrived(k, gall_ref.at[0], (sgu.at[2], rgu.at[2]))
        if k == 0:
            line.arrived(k, hp_ref.at[last], (shd.at[2], rhd.at[2]))
            line.arrived(k, gall_ref.at[last], (sgd.at[2], rgd.at[2]))

    line.each(sixth)
    line.leave()


def middle_part(route, dh_ref, gt_ref, sm_ref, wrc_ref, x1_ref, gain_ref, g_ref, h2_ref, w_ref, o_ref, gv_ref,
                dx_ref, da_ref, do_ref, delta_ref, dres_ref, small_ref):
    rows = x1_ref.shape[0]
    dgf = dh_ref[rows : rows + SPARE, 0:rows]
    dh = dh_ref[0:rows, :]
    dgate = jnp.concatenate([dgf[0:EXPERTS] + dgf[EXPERTS:], sm_ref[EXPERTS:SPARE]], axis=0)
    expert = iota((SPARE, rows), 0)
    named0, named1 = expert == route[0:1], expert == route[1:2]
    g0, g1 = gt_ref[0:1], gt_ref[1:2]
    d0 = jnp.sum(jnp.where(named0, dgate, 0.0), axis=0, keepdims=True)
    d1 = jnp.sum(jnp.where(named1, dgate, 0.0), axis=0, keepdims=True)
    inner = g0 * d0 + g1 * d1
    dz = jnp.where(named0, g0 * (d0 - inner), jnp.where(named1, g1 * (d1 - inner), 0.0))
    dres_ref[...] = dz
    dz = jnp.where(expert < 12, dz, sm_ref[...])
    zh, zm, zl = split3(dz)
    wh, wm, wl = split3(wrc_ref[...])
    dh = dh + (mm(zh, wl, TN) + mm(zl, wh, TN) + mm(zm, wm, TN) + mm(zh, wm, TN) + mm(zm, wh, TN) + mm(zh, wh, TN))
    h = h2_ref[...]
    small_ref[0:SPARE, :] = mm(zl, h, NN) + mm(zm, h, NN) + mm(zh, h, NN)
    x1 = x1_ref[...]
    r = lax.rsqrt(jnp.mean(x1 * x1, axis=1, keepdims=True) + EPSILON)
    xr = x1 * r
    grad_gain = jnp.sum(dh * xr, axis=0, keepdims=True)
    gv = gv_ref[...]
    small_ref[SPARE : SPARE + 8, :] = jnp.concatenate([gv[0:2], grad_gain, gv[3:8]], axis=0)
    scaled = dh * gain_ref[...]
    dx = g_ref[...].astype(F32) + r * (scaled - xr * jnp.mean(xr * scaled, axis=1, keepdims=True))
    dx_ref[...] = dx
    da = dx.astype(BF16)
    da_ref[...] = da
    do = mm(da, w_ref[:, 3 * D : 4 * D], NN).astype(BF16)
    do_ref[...] = do
    high, low = split2(do.astype(F32) * o_ref[...].astype(F32))
    heads = pick(iota((SPARE, D), 1) // HEAD_DIM == iota((SPARE, D), 0))
    delta_ref[...] = mm(heads, high, NT) + mm(heads, low, NT)


def backward_body(size, back_ref, out_ref, dhl_ref, gt_ref, sm_ref, routes_ref, wrc_ref, xm_ref, gain_ref, g_ref, hp_ref, w_ref,
                  o_ref, gv_ref, q_ref, k_ref, v_ref, lse_ref, start_ref, cos_ref, sin_ref, xl_ref,
                  dx_ref, da_ref, dres_ref, small_ref, dq_ref, dk_ref, dv_ref, y_ref,
                  bias_ref, dkf_ref, dvf_ref, dh_ref, do_ref, delta_ref, bu_ref, bd_ref, fu_ref, fd_ref,
                  sbu, rbu, sbd, rbd, sfu, rfu, sfd, rfd):
    rows = xm_ref.shape[0]
    packed = rows + SPARE
    cut = 272
    pieces = (slice(0, cut), slice(cut, packed))
    line = Line(size)
    t = line.place
    last = size - 1
    line.enter()

    def add_rows(held, mine):
        def one(i, _):
            at = pl.ds(pl.multiple_of(i * 16, 16), 16)
            held[at, :] = (held[at, :].astype(F32) + mine[at, :].astype(F32)).astype(BF16)
            return 0

        lax.fori_loop(0, held.shape[0] // 16, one, 0)

    def handle(k, way, dest, part, index, mine_ref, up_ref, down_ref, ups, downs):
        slot = dest - 1 if way == 1 else dest
        first = k == (0 if way == 1 else last)
        mine = mine_ref.at[dest, part]

        def refs():
            held = (up_ref if way == 1 else down_ref).at[slot, part]
            sems = tuple(s.at[slot, index] for s in (ups if way == 1 else downs))
            return mine_ref.at[dest, part] if first else held, held, sems

        _, held, sems = refs()
        if not first:
            line.arrived(k, held, sems)
        if dest != k:
            if not first:
                add_rows(held, mine)
            line.send(k, k + way, refs)

    def sum_back(k, opening):
        for time, way, dest in sum_events(size, k):
            if (time == 0) != opening:
                continue
            for index, part in enumerate(pieces):
                handle(k, way, dest, part, index, back_ref, bu_ref, bd_ref, (sbu, rbu), (sbd, rbd))

    def sum_out(k, now):
        for time, way, dest in sum_events(size, k):
            if time == now:
                handle(k, way, dest, slice(0, rows), 0, out_ref, fu_ref, fd_ref, (sfu, rfu), (sfd, rfd))

    line.each(lambda k: (sum_back(k, True), sum_out(k, 0), None)[2])
    line.each(lambda k: sum_back(k, False))
    dh_ref[...] = back_ref[t].astype(F32)

    @pl.when(t > 0)
    def _():
        dh_ref[...] += bu_ref[t - 1].astype(F32)

    @pl.when(t < last)
    def _():
        dh_ref[...] += bd_ref[t].astype(F32)

    dh_ref[0:rows, :] += dhl_ref[...]
    middle_part(routes_ref[t], dh_ref, gt_ref, sm_ref, wrc_ref, xm_ref, gain_ref, g_ref, hp_ref.at[t, 0:rows], w_ref, o_ref, gv_ref,
                dx_ref, da_ref, do_ref, delta_ref, dres_ref, small_ref)
    line.each(lambda k: sum_out(k, 1))

    block = 256
    window = LONGEST + block
    lane = iota((1, 128), 1) // HEAD_DIM
    for rb in range(rows // block):
        first = rb * block
        bias_ref[rb] = key_bias(start_ref[:, first : first + block], block, first, LONGEST)

    def pair(i, _):
        lanes = pl.ds(pl.multiple_of(i * 128, 128), 128)
        for rb in range(rows // block):
            first = rb * block
            k = k_ref[first : first + window, lanes]
            v = v_ref[first : first + window, lanes]
            kt = k.T
            q = q_ref[first : first + block, lanes]
            do = do_ref[first : first + block, lanes]
            dk = jnp.zeros((window, 128), F32)
            dv = jnp.zeros((window, 128), F32)
            parts = []
            for half in range(2):
                qm = jnp.where(lane == half, q, jnp.zeros_like(q))
                dom = jnp.where(lane == half, do, jnp.zeros_like(do))
                head = pl.ds(i * 2 + half, 1)
                s = mm(k, qm, NT) * (SCORE_SCALE * LOG2E) + bias_ref[rb]
                p = jnp.exp2(s - lse_ref[head, first : first + block])
                dp = mm(v, dom, NT)
                ds = (p * (dp - delta_ref[head, first : first + block])).astype(BF16)
                dv = dv + mm(p.astype(BF16), dom, NN)
                dk = dk + mm(ds, qm, NN)
                parts.append(mm(kt[half * HEAD_DIM : (half + 1) * HEAD_DIM], ds, NN))
            dq = jnp.concatenate(parts, axis=0).T * SCORE_SCALE
            at = slice(2 * rows + first, 2 * rows + first + block)
            dq_ref[first : first + block, lanes] = (dq * cos_ref[at, :] - turn(dq) * sin_ref[at, :]).astype(BF16)
            if first == 0:
                dkf_ref[0:window, :] = dk
                dvf_ref[0:window, :] = dv
            else:
                old = window - block
                dkf_ref[first : first + old, :] += dk[0:old]
                dvf_ref[first : first + old, :] += dv[0:old]
                dkf_ref[first + old : first + window, :] = dk[old:]
                dvf_ref[first + old : first + window, :] = dv[old:]
        dk = dkf_ref[...] * SCORE_SCALE
        dk_ref[:, lanes] = (dk * cos_ref[...] - turn(dk) * sin_ref[...]).astype(BF16)
        dv_ref[:, lanes] = dvf_ref[...].astype(BF16)
        return 0

    lax.fori_loop(0, HEADS // 4, pair, 0)
    line.each(lambda k: sum_out(k, 2))
    lax.fori_loop(HEADS // 4, HEADS // 2, pair, 0)
    line.each(lambda k: sum_out(k, 3))
    xl_ref[...] += out_ref[t].astype(F32)

    @pl.when(t > 0)
    def _():
        xl_ref[...] += fu_ref[t - 1].astype(F32)

    @pl.when(t < last)
    def _():
        xl_ref[...] += fd_ref[t].astype(F32)

    y_ref[...] = xl_ref[...].astype(BF16)
    line.leave()


def grads_body(size, x0_ref, x1_ref, x2_ref, h_ref, dq_ref, dk_ref, dv_ref, da_ref, o_ref, w_ref, dx_ref, gain_ref,
               gw_ref, gpart_ref, out_ref, d0_ref, d1_ref, d2_ref, ra_ref, rb_ref, sems_s, sems_r):
    rows = x0_ref.shape[0]
    line = Line(size)
    last = size - 1
    block = 256
    line.enter()

    def hidden(c, d_ref):
        def one(i, _):
            at = pl.ds(pl.multiple_of(i * block, block), block)
            to = pl.ds(pl.multiple_of(c * rows + i * block, block), block)
            total = mm(dk_ref[to, :], w_ref[:, D : 2 * D], NT) + mm(dv_ref[to, :], w_ref[:, 2 * D : 3 * D], NT)
            if c == 2:
                total = total + mm(dq_ref[at, :], w_ref[:, 0:D], NT)
            d_ref[at, :] = total.astype(d_ref.dtype)
            return 0

        lax.fori_loop(0, rows // block, one, 0)

    def gain_of(x_ref, d_ref):
        x = x_ref[...].astype(F32)
        r = lax.rsqrt(jnp.mean(x * x, axis=1, keepdims=True) + EPSILON)
        return jnp.sum(d_ref[...].astype(F32) * x * r, axis=0, keepdims=True)

    hidden(0, d2_ref)

    def first(k):
        if k > 1:
            line.send(k, k - 1, lambda: (d2_ref, ra_ref, (sems_s.at[0], sems_r.at[0])))

    line.each(first)
    hidden(1, d1_ref)
    gain = gain_of(x2_ref, d2_ref) + gain_of(x1_ref, d1_ref)
    h = h_ref[...]

    def weight(column, left, right_ref):
        for c in range(D // 256):
            cols = slice(c * 256, (c + 1) * 256)
            gw_ref[:, column * D + c * 256 : column * D + c * 256 + 256] = mm(left, right_ref[:, cols], TN).astype(BF16)

    weight(1, h, dk_ref)

    def second(k):
        if 0 < k < last:
            line.arrived(k, ra_ref, (sems_s.at[0], sems_r.at[0]))
            d1_ref[...] = (d1_ref[...].astype(F32) + ra_ref[...].astype(F32)).astype(BF16)
        if k > 0:
            line.send(k, k - 1, lambda: (d1_ref, rb_ref, (sems_s.at[1], sems_r.at[1])))

    line.each(second)
    hidden(2, d0_ref)
    gpart_ref[...] = jnp.broadcast_to(gain + gain_of(x0_ref, d0_ref), (8, D))
    weight(2, h, dv_ref)
    weight(0, h[2 * rows :], dq_ref)
    weight(3, da_ref[...], o_ref)

    def third(k):
        if k < last:
            line.arrived(k, rb_ref, (sems_s.at[1], sems_r.at[1]))
            d0_ref[...] += rb_ref[...].astype(F32)

    line.each(third)
    x = x0_ref[...].astype(F32)
    r = lax.rsqrt(jnp.mean(x * x, axis=1, keepdims=True) + EPSILON)
    xr = x * r
    scaled = d0_ref[...] * gain_ref[...]
    out_ref[...] = (dx_ref[...] + r * (scaled - xr * jnp.mean(xr * scaled, axis=1, keepdims=True))).astype(BF16)
    line.leave()


def finish_body(n_dp, size, x0_ref, x1_ref, x2_ref, h_ref, dq_ref, dk_ref, dv_ref, da_ref, o_ref, w_ref, dx_ref, gain_ref,
                y_ref, small_ref, pos_ref,
                yo_ref, go_ref, gw_ref, sum_ref,
                d0_ref, d1_ref, d2_ref, ra_ref, rb_ref, out_ref, yr_ref, gr_ref, part_ref, r1_ref, r2_ref, r3_ref,
                zs_ref, zr_ref, cur_ref, got_ref,
                sems_s, sems_r, sy, ry, sg, rg, s1, r1, s2, r2, s3, r3, sz, rz, sb, rb):
    rows = x0_ref.shape[0]
    share = rows // n_dp
    line = Line(size)
    last = size - 1
    block = 256
    net = Peers()
    d, t = net.d, net.t
    place = pick(iota((rows, rows), 0) == pos_ref[...])
    about, along = around(d, n_dp), around(t, size)
    net.enter([{"dp": to} for _, to, _ in about] + [{"tensor": to} for _, to, _ in along])

    def scatter(src_ref, dst_ref, sems):
        for j, to, _ in about:
            net.send({"dp": to}, src_ref.at[to], dst_ref.at[d], (sems[0].at[j - 1], sems[1].at[j - 1]))
        dst_ref[d] = src_ref[d]

    def gathered(dst_ref, sems):
        for j, _, source in about:
            held = dst_ref.at[source]
            net.copy({"dp": source}, held, held, (sems[0].at[j - 1], sems[1].at[j - 1])).wait_recv()

    scatter(y_ref, yr_ref, (sy, ry))

    def hidden(c, d_ref):
        def one(i, _):
            at = pl.ds(pl.multiple_of(i * block, block), block)
            to = pl.ds(pl.multiple_of(c * rows + i * block, block), block)
            total = mm(dk_ref[to, :], w_ref[:, D : 2 * D], NT) + mm(dv_ref[to, :], w_ref[:, 2 * D : 3 * D], NT)
            if c == 2:
                total = total + mm(dq_ref[at, :], w_ref[:, 0:D], NT)
            d_ref[at, :] = total.astype(d_ref.dtype)
            return 0

        lax.fori_loop(0, rows // block, one, 0)

    def gain_of(x_ref, d_ref):
        x = x_ref[...].astype(F32)
        r = lax.rsqrt(jnp.mean(x * x, axis=1, keepdims=True) + EPSILON)
        return jnp.sum(d_ref[...].astype(F32) * x * r, axis=0, keepdims=True)

    core, x, y = lax.rem(d, 2), lax.rem(d // 2, 2), d // 4
    there = ({"dp": flip(d, 2)}, {"dp": flip(d, 4)})
    deep = D // n_dp

    def weight(u, left, right_ref):
        for c in range(D // 256):
            cols = slice(c * 256, (c + 1) * 256)
            value = mm(left, right_ref[:, cols], TN).astype(BF16)
            part_ref[u, :, :, cols] = value.reshape(n_dp, deep, 256)
        for j in range(4):
            net.send({"dp": flip(d, 1)}, part_ref.at[u, 2 * j + 1 - core], r1_ref.at[u, j], (s1.at[u, j], r1.at[u, j]))

    def add(u, j, arrived):
        spot = 2 * j + core
        part_ref[u, spot] = (part_ref[u, spot].astype(F32) + arrived[...].astype(F32)).astype(BF16)

    def chips(u):
        if u % 2 == 0:
            first = (there[0], [2 * i + 1 - x for i in range(2)], [2 * i + x for i in range(2)])
            return first, (there[1], 2 * (1 - y) + x)
        first = (there[1], [2 * (1 - y) + i for i in range(2)], [2 * y + i for i in range(2)])
        return first, (there[0], 2 * y + 1 - x)

    def halve(u):
        for j in range(4):
            held = r1_ref.at[u, j]
            net.copy({"dp": flip(d, 1)}, held, held, (s1.at[u, j], r1.at[u, j])).wait_recv()
            add(u, j, held)
        where, theirs, _ = chips(u)[0]
        for i in range(2):
            net.send(where, part_ref.at[u, 2 * theirs[i] + core], r2_ref.at[u, i], (s2.at[u, i], r2.at[u, i]))

    def quarter(u):
        (where, _, mine), (after, spot) = chips(u)
        for i in range(2):
            held = r2_ref.at[u, i]
            net.copy(where, held, held, (s2.at[u, i], r2.at[u, i])).wait_recv()
            add(u, mine[i], held)
        net.send(after, part_ref.at[u, 2 * spot + core], r3_ref.at[u], (s3.at[u], r3.at[u]))

    def own(u):
        after = chips(u)[1][0]
        held = r3_ref.at[u]
        net.copy(after, held, held, (s3.at[u], r3.at[u])).wait_recv()
        value = part_ref[u, d].astype(F32) + held[...].astype(F32)
        wide_share = D // size
        for p in range(size):
            zs_ref[u, p] = value[:, p * wide_share : (p + 1) * wide_share].astype(BF16)
        for j, to, _ in along:
            net.send({"tensor": to}, zs_ref.at[u, to], zr_ref.at[u, j - 1], (sz.at[u, j - 1], rz.at[u, j - 1]))

    def whole(u):
        total = zs_ref[u, t].astype(F32)
        for j, _, source in along:
            held = zr_ref.at[u, j - 1]
            net.copy({"tensor": source}, held, held, (sz.at[u, j - 1], rz.at[u, j - 1])).wait_recv()
            total = total + held[...].astype(F32)
        gw_ref[u] = total

    steps = [("dp", bit) for bit in (1, 2, 4, 8) if bit < n_dp] + [("tensor", bit) for bit in (1, 2, 4, 8) if bit < size]

    def small_out(i):
        axis, bit = steps[i]
        mine = t if axis == "tensor" else d
        net.send({axis: flip(mine, bit)}, cur_ref.at[i], got_ref.at[i], (sb.at[i], rb.at[i]))

    def small_in(i):
        axis, bit = steps[i]
        mine = t if axis == "tensor" else d
        held = got_ref.at[i]
        net.copy({axis: flip(mine, bit)}, held, held, (sb.at[i], rb.at[i])).wait_recv()
        total = cur_ref[i] + held[...]
        if i + 1 < len(steps):
            cur_ref[i + 1] = total
            small_out(i + 1)
        else:
            sum_ref[...] = total

    hidden(0, d2_ref)

    def first(k):
        if k > 1:
            line.send(k, k - 1, lambda: (d2_ref, ra_ref, (sems_s.at[0], sems_r.at[0])))

    line.each(first)
    hidden(1, d1_ref)

    def second(k):
        if k == last:
            line.send(k, k - 1, lambda: (d1_ref, rb_ref, (sems_s.at[1], sems_r.at[1])))

    line.each(second)
    h = h_ref[...]
    weight(0, h, dk_ref)
    gain = gain_of(x2_ref, d2_ref) + gain_of(x1_ref, d1_ref)
    weight(1, h, dv_ref)
    halve(0)
    hidden(2, d0_ref)
    gain = gain + gain_of(x0_ref, d0_ref)
    rest = small_ref.shape[0]
    cur_ref[0, 0:rest, :] = small_ref[...]
    cur_ref[0, rest : rest + 8, :] = jnp.broadcast_to(gain, (8, D))
    small_out(0)
    halve(1)

    def third(k):
        if 0 < k < last:
            line.arrived(k, ra_ref, (sems_s.at[0], sems_r.at[0]))
            d1_ref[...] = (d1_ref[...].astype(F32) + ra_ref[...].astype(F32)).astype(BF16)
            line.send(k, k - 1, lambda: (d1_ref, rb_ref, (sems_s.at[1], sems_r.at[1])))

    line.each(third)
    weight(2, h[2 * rows :], dq_ref)
    small_in(0)
    weight(3, da_ref[...], o_ref)
    quarter(0)
    quarter(1)
    halve(2)
    small_in(1)
    halve(3)
    own(0)
    own(1)
    gathered(yr_ref, (sy, ry))
    yo_ref[...] = mm(place, yr_ref[...].reshape(rows, D), TN).astype(BF16)
    quarter(2)
    quarter(3)
    small_in(2)
    own(2)
    own(3)

    def fourth(k):
        if k < last:
            line.arrived(k, rb_ref, (sems_s.at[1], sems_r.at[1]))
            d0_ref[...] += rb_ref[...].astype(F32)

    line.each(fourth)
    xv = x0_ref[...].astype(F32)
    r = lax.rsqrt(jnp.mean(xv * xv, axis=1, keepdims=True) + EPSILON)
    xr = xv * r
    scaled = d0_ref[...] * gain_ref[...]
    value = dx_ref[...] + r * (scaled - xr * jnp.mean(xr * scaled, axis=1, keepdims=True))
    out_ref[...] = value.astype(BF16).reshape(n_dp, share, D)
    scatter(out_ref, gr_ref, (sg, rg))
    for i in range(3, len(steps)):
        small_in(i)
    for u in range(4):
        whole(u)
    gathered(gr_ref, (sg, rg))
    go_ref[...] = mm(place, gr_ref[...].reshape(rows, D), TN).astype(BF16)
    line.leave()
    net.leave()


def experts_body(ff, chunks, cnt_ref, h_refs, g_refs, slot_ref, w_ref, o_refs, d_refs, gw_ref,
                 xbuf, gbuf, cbuf, onehot, fbuf, dbuf, gacc, gates, dgrow, off_ref, base_ref, nt_ref):
    rows = slot_ref.shape[2]
    e = pl.program_id(0)

    def match(j, expert, tile):
        slots = slot_ref[j, pl.ds(expert, 1), :]
        return (iota((TILE, rows), 0) + tile * TILE) == slots

    def store_rows(at, count, hit, x, gs, gate_row):
        to = pl.ds(pl.multiple_of(at, 16), TILE)
        keep = iota((TILE, 1), 0) < count
        col = jnp.sum(jnp.where(hit, gate_row, 0.0), axis=1, keepdims=True)
        xbuf[to, :] = jnp.where(keep, x, xbuf[to, :].astype(F32)).astype(BF16)
        gbuf[to, :] = jnp.where(keep, gs, gbuf[to, :].astype(F32)).astype(BF16)
        cbuf[to, :] = jnp.where(keep, jnp.broadcast_to(col, (TILE, 128)), cbuf[to, :])

    def round16(n):
        return ((n + 15) // 16) * 16

    @pl.when(e == 0)
    def _gather():
        at = jnp.int32(0)
        for ex in range(EXPERTS):
            base_ref[ex] = at
            here = at
            for j in range(chunks):
                off_ref[j * EXPERTS + ex] = here
                here = here + round16(cnt_ref[j * EXPERTS + ex])
            tiles = (here - at + (ROWS - 1)) // ROWS
            nt_ref[ex] = tiles
            tail = pl.ds(pl.multiple_of(here, 16), ROWS)
            xbuf[tail, :] = jnp.zeros((ROWS, D), BF16)
            gbuf[tail, :] = jnp.zeros((ROWS, D), BF16)
            cbuf[tail, :] = jnp.zeros((ROWS, 128), F32)
            at = at + tiles * ROWS
        for j in range(chunks):
            gates[...] = h_refs[j, rows : rows + SPARE, 0:rows].astype(F32)

            def two(i, _, j=j):
                hits = [match(j, 2 * i + half, 0) for half in range(2)]
                sel = jnp.concatenate([pick(hit) for hit in hits], axis=0)
                x = mm(sel, h_refs[j, 0:rows, :], NN)
                gs = mm(sel, g_refs[j], NN)
                for half in range(2):
                    ex = 2 * i + half
                    count = round16(jnp.minimum(cnt_ref[j * EXPERTS + ex], TILE))
                    part = slice(half * TILE, (half + 1) * TILE)
                    store_rows(off_ref[j * EXPERTS + ex], count, hits[half], x[part], gs[part], gates[pl.ds(ex, 1), :])
                return 0

            lax.fori_loop(0, EXPERTS // 2, two, 0)

            def rare(ex, _, j=j):
                def more(tile, _):
                    hit = match(j, ex, tile)
                    sel = pick(hit)
                    count = round16(jnp.minimum(cnt_ref[j * EXPERTS + ex] - tile * TILE, TILE))
                    store_rows(
                        off_ref[j * EXPERTS + ex] + tile * TILE,
                        count,
                        hit,
                        mm(sel, h_refs[j, 0:rows, :], NN),
                        mm(sel, g_refs[j], NN),
                        gates[pl.ds(ex, 1), :],
                    )
                    return 0

                return lax.fori_loop(1, (cnt_ref[j * EXPERTS + ex] + (TILE - 1)) // TILE, more, 0)

            lax.fori_loop(0, EXPERTS, rare, 0)

    gacc[...] = jnp.zeros_like(gacc)

    def tile_step(m, _):
        at = pl.ds(pl.multiple_of(base_ref[e] + m * ROWS, 16), ROWS)
        x = xbuf[at, :]
        gs = gbuf[at, :].astype(F32)
        gate = wide(cbuf[at, :])
        u = mm(x, w_ref[:, 0:ff], NN)
        up = mm(x, w_ref[:, ff : 2 * ff], NN)
        sig = jax.nn.sigmoid(u)
        silu = u * sig
        act = (silu * up).astype(BF16)
        f = mm(act, w_ref[:, 2 * ff : 3 * ff], NT)
        cbuf[at, :] = jnp.broadcast_to(jnp.sum(gs * f, axis=1, keepdims=True), (ROWS, 128))
        gbuf[at, :] = (f * gate).astype(BF16)
        df = (gs * gate).astype(BF16)
        dact = mm(df, w_ref[:, 2 * ff : 3 * ff], NN)
        dup = (dact * silu).astype(BF16)
        du = (dact * up * sig * (1.0 + u * (1.0 - sig))).astype(BF16)
        xbuf[at, :] = (mm(du, w_ref[:, 0:ff], NT) + mm(dup, w_ref[:, ff : 2 * ff], NT)).astype(BF16)
        gacc[:, 0:ff] += mm(x, du, TN)
        gacc[:, ff : 2 * ff] += mm(x, dup, TN)
        gacc[:, 2 * ff : 3 * ff] += mm(df, act, TN)
        return 0

    lax.fori_loop(0, nt_ref[e], tile_step, 0)
    gw_ref[...] = gacc[...].astype(BF16)

    @pl.when(e == EXPERTS - 1)
    def _scatter():
        for j in range(chunks):
            def take(ex, _, j=j):
                at = pl.ds(pl.multiple_of(off_ref[j * EXPERTS + ex], 16), TILE)
                to = pl.ds(pl.multiple_of(ex * TILE, 16), TILE)
                hit = match(j, ex, 0)
                onehot[to, :] = pick(hit)
                fbuf[to, :] = gbuf[at, :]
                dbuf[to, :] = xbuf[at, :]
                col = jnp.concatenate([cbuf[at, :]] * (rows // 128), axis=1)
                dgrow[pl.ds(ex, 1), :] = jnp.sum(jnp.where(hit, col, 0.0), axis=0, keepdims=True)
                return 0

            lax.fori_loop(0, EXPERTS, take, 0)
            gacc[0:rows, 0:D] = mm(onehot[...], fbuf[...], TN)
            gacc[0:rows, D : 2 * D] = mm(onehot[...], dbuf[...], TN)

            def rare(ex, _, j=j):
                def more(tile, _):
                    at = pl.ds(pl.multiple_of(off_ref[j * EXPERTS + ex] + tile * TILE, 16), TILE)
                    hit = match(j, ex, tile)
                    sel = pick(hit)
                    gacc[0:rows, 0:D] += mm(sel, gbuf[at, :], TN)
                    gacc[0:rows, D : 2 * D] += mm(sel, xbuf[at, :], TN)
                    col = jnp.concatenate([cbuf[at, :]] * (rows // 128), axis=1)
                    dgrow[pl.ds(ex, 1), :] += jnp.sum(jnp.where(hit, col, 0.0), axis=0, keepdims=True)
                    return 0

                return lax.fori_loop(1, (cnt_ref[j * EXPERTS + ex] + (TILE - 1)) // TILE, more, 0)

            lax.fori_loop(0, EXPERTS, rare, 0)
            o_refs[j] = gacc[0:rows, 0:D].astype(BF16)
            d_refs[j, 0:rows, :] = gacc[0:rows, D : 2 * D].astype(BF16)
            total = dgrow[...]
            high = total.astype(BF16).astype(F32)
            both = jnp.concatenate([high, total - high], axis=0)
            d_refs[j, rows : rows + SPARE, :] = jnp.concatenate(
                [both, jnp.zeros((SPARE, D - rows), F32)], axis=1
            ).astype(BF16)


def experts_call(counts, hs, gs, slots, weights, ff):
    chunks, rows = gs.shape[:2]
    width = 3 * ff
    most = (rows + 15 * chunks + ROWS - 1) // ROWS * ROWS * EXPERTS + ROWS
    whole = lambda shape: pl.BlockSpec(shape, lambda e: (0,) * len(shape), pipeline_mode=pl.Buffered(1))
    return pl.pallas_call(
        functools.partial(experts_body, ff, chunks),
        name="experts",
        grid=(EXPERTS,),
        in_specs=[smem(), whole(hs.shape), whole(gs.shape), whole(slots.shape), pl.BlockSpec((D, width), lambda e: (0, e))],
        out_specs=[whole(gs.shape), whole(hs.shape), pl.BlockSpec((D, width), lambda e: (0, e))],
        out_shape=[
            jax.ShapeDtypeStruct(gs.shape, BF16),
            jax.ShapeDtypeStruct(hs.shape, BF16),
            jax.ShapeDtypeStruct((D, EXPERTS * width), BF16),
        ],
        scratch_shapes=[
            pltpu.VMEM((most, D), BF16),
            pltpu.VMEM((most, D), BF16),
            pltpu.VMEM((most, 128), F32),
            pltpu.VMEM((EXPERTS * TILE, rows), BF16),
            pltpu.VMEM((EXPERTS * TILE, D), BF16),
            pltpu.VMEM((EXPERTS * TILE, D), BF16),
            pltpu.VMEM((D, width), F32),
            pltpu.VMEM((SPARE, rows), F32),
            pltpu.VMEM((EXPERTS, rows), F32),
            pltpu.SMEM((chunks * EXPERTS,), I32),
            pltpu.SMEM((EXPERTS,), I32),
            pltpu.SMEM((EXPERTS,), I32),
        ],
        compiler_params=pltpu.CompilerParams(
            dimension_semantics=("arbitrary",), vmem_limit_bytes=VMEM_CAP
        ),
    )(counts, hs, gs, slots, weights)


def body(tokens, cotangent, deal, lengths, routes, gate_residual, w_qkv, w_out, w_gate_up, w_down,
         norm_gain_attn, norm_gain_moe, w_router, w_const, v_const):
    rows = tokens.shape[0]
    n_dp, n_t = lax.axis_size("dp"), lax.axis_size("tensor")
    t = lax.axis_index("tensor")
    ff = w_down.shape[2]
    d_here = w_qkv.shape[0]

    def swap(v, j):
        return lax.ppermute(v, "tensor", [(i, i ^ j) for i in range(n_t)])

    def place_in(parts):
        stacked = jnp.stack(parts)
        return jnp.stack([lax.dynamic_index_in_dim(stacked, t ^ i, 0, keepdims=False) for i in range(n_t)], axis=2)

    fast = n_dp == 8 and d_here % 16 == 0 and rows % 128 == 0
    attn_shard = jnp.concatenate([w_qkv, w_out[:, None, :]], axis=1)
    if not fast:
        attn_shard = place_in([attn_shard] + [swap(attn_shard, j) for j in range(1, n_t)]).reshape(d_here, 4 * D)
        w_attn = lax.all_gather(attn_shard, "dp", axis=0, tiled=True)
    ff_shard = jnp.concatenate([w_gate_up.reshape(d_here, EXPERTS, 2 * ff), w_down], axis=2)

    routes_t = routes.reshape(n_t, rows, 2).transpose(0, 2, 1)
    row, ext = (rows, D), (3 * rows, D)
    every, every_packed = (n_t, rows, D), (n_t, rows + SPARE, D)
    xs, gs, pos, slots, counts = call(
        functools.partial(deal_body, n_dp),
        "deal",
        [(row, BF16), (row, BF16), ((1, rows), I32), ((n_t, EXPERTS, rows), I32), ((n_t, EXPERTS, 128), I32)],
        [deal.reshape(1, rows), tokens, cotangent, routes_t],
    )
    counts = counts[:, :, 0].reshape(n_t * EXPERTS)
    share = rows // n_dp
    if fast:
        parts = (n_dp, share, D)
    else:
        parts = (1, rows, D)
        x0 = lax.all_to_all(xs, "dp", split_axis=0, concat_axis=0, tiled=True)
        g0 = lax.all_to_all(gs, "dp", split_axis=0, concat_axis=0, tiled=True)

    half = HEAD_DIM // 2
    rates = jnp.asarray(np.tile(10000.0 ** (np.arange(half) / -half), 4).reshape(1, 128), F32)
    gain_attn, gain_moe = norm_gain_attn.reshape(1, D), norm_gain_moe.reshape(1, D)
    window = LONGEST + 256
    res_t = jnp.concatenate([gate_residual.T, jnp.zeros((4, rows), F32)], axis=0)
    wrc = jnp.concatenate([w_router.T, w_const.transpose(0, 2, 1).reshape(4, D)], axis=0)
    v8 = jnp.concatenate([v_const, jnp.zeros((6, D), F32)], axis=0)
    dma = lambda *shape: pltpu.SemaphoreType.DMA(shape)
    found = [(parts, BF16), (parts, BF16), ((3 * rows, 128), F32), ((3 * rows, 128), F32), ((1, rows), I32)]
    if fast:
        x0, g0, w_attn, x1, x2, cos, sin, start = call(
            functools.partial(opening_body, n_dp, n_t),
            "opening",
            [(parts, BF16), (parts, BF16), ((n_dp, d_here, 4 * D), BF16)] + found,
            [lengths[0], xs.reshape(parts), gs.reshape(parts), attn_shard.transpose(1, 0, 2), rates],
            scalars=1,
            scratch=[pltpu.VMEM((n_t, 4, d_here, D // n_t), BF16)] + [dma(n_t - 1)] * 2 + [dma(n_dp - 1)] * 4
            + [dma(2)] * 2 + [dma(2, 2)] * 2 + [dma(n_dp // 2)] * 2 + [dma(2)] * 2,
            meet=3,
        )
        x0, ff_shard = lax.optimization_barrier((x0, ff_shard))
        given, more = [x0, g0, w_attn, x1, x2, cos, sin, start], []
    else:
        given, more = [lengths[0], rates, x0.reshape(parts), g0.reshape(parts), w_attn.reshape(1, D, 4 * D)], found
    w_ff = lax.all_gather(ff_shard.reshape(d_here, EXPERTS * 3 * ff), "dp", axis=0, tiled=True)
    results = call(
        functools.partial(forward_body, fast, n_t),
        "forward",
        more
        + [(ext, BF16), (row, BF16), (ext, BF16), (ext, BF16), (row, BF16), ((SPARE, rows), F32),
           (row, F32), (every_packed, BF16), ((n_t,) + parts, BF16), ((8, rows), F32), (row, F32), (row, F32), ((SPARE, rows), F32),
           ((8, D), F32)],
        given + [gain_attn, gain_moe, res_t, wrc, routes_t, v8],
        scalars=0 if fast else 1,
        scratch=[pltpu.VMEM((window, 256), F32), dma(2), dma(2)] + [dma(3)] * 8,
        meet=0,
    )
    if fast:
        x0, g0, w_attn = x0.reshape(row), g0.reshape(row), w_attn.reshape(D, 4 * D)
    else:
        x1, x2, cos, sin, start = results[:5]
        results = results[5:]
    h, q, k, v, o, lse, xm, hp_all, g_all, gt, xl, dhl, sm, gv = results
    x1, x2, g_all = x1.reshape(row), x2.reshape(row), g_all.reshape(every)

    out_all, back_all, gw_ff = experts_call(counts, hp_all, g_all, slots, w_ff, ff)
    ff_sum = lax.psum_scatter(gw_ff, "dp", scatter_dimension=0, tiled=True)

    dx, da, dres, small, dq, dk, dv, result = call(
        functools.partial(backward_body, n_t),
        "backward",
        [(row, F32), (row, BF16), ((SPARE, rows), F32), ((SPARE + 8, D), F32), (row, BF16), (ext, BF16), (ext, BF16), (row, BF16)],
        [back_all, out_all, dhl, gt, sm, routes_t, wrc, xm, gain_moe, g0, hp_all, w_attn, o, gv, q, k, v, lse, start, cos, sin, xl],
        scratch=[pltpu.VMEM((rows // 256, window, 256), F32), pltpu.VMEM((3 * rows, 128), F32), pltpu.VMEM((3 * rows, 128), F32),
                 pltpu.VMEM((rows + SPARE, D), F32), pltpu.VMEM(row, BF16), pltpu.VMEM((SPARE, rows), F32)]
        + [pltpu.VMEM((n_t - 1, rows + SPARE, D), BF16)] * 2 + [pltpu.VMEM((n_t - 1, rows, D), BF16)] * 2
        + [dma(n_t - 1, 2)] * 4 + [dma(n_t - 1, 1)] * 4,
        meet=1,
    )
    if fast:
        units = 4
        piece = (d_here, D)
        hops = 3 + (n_t - 1).bit_length()
        output, grad_tokens, attn_parts, small_all = call(
            functools.partial(finish_body, n_dp, n_t),
            "finish",
            [(row, BF16), (row, BF16), ((units, d_here, D // n_t), F32), ((SPARE + 16, D), F32)],
            [x0, x1, x2, h, dq, dk, dv, da, o, w_attn, dx, gain_attn, result.reshape(n_dp, share, D), small, pos],
            scratch=[pltpu.VMEM(row, F32)] + [pltpu.VMEM(row, BF16)] * 4 + [pltpu.VMEM((n_dp, share, D), BF16)] * 3
            + [pltpu.VMEM((units, n_dp) + piece, BF16), pltpu.VMEM((units, 4) + piece, BF16), pltpu.VMEM((units, 2) + piece, BF16),
               pltpu.VMEM((units,) + piece, BF16), pltpu.VMEM((units, n_t, d_here, D // n_t), BF16),
               pltpu.VMEM((units, n_t - 1, d_here, D // n_t), BF16)]
            + [pltpu.VMEM((hops, SPARE + 16, D), F32)] * 2
            + [dma(2)] * 2 + [dma(n_dp - 1)] * 4 + [dma(units, 4)] * 2 + [dma(units, 2)] * 2 + [dma(units)] * 2
            + [dma(units, n_t - 1)] * 2 + [dma(hops)] * 2,
            meet=2,
        )
        gain_all = small_all[SPARE + 8]
        attn_own = jnp.stack([attn_parts[2], attn_parts[0], attn_parts[1], attn_parts[3]], axis=1)
    else:
        back_out = lax.all_to_all(result, "dp", split_axis=0, concat_axis=0, tiled=True)
        gw_attn, gain_part, d_start = call(
            functools.partial(grads_body, n_t),
            "grads",
            [((D, 4 * D), BF16), ((8, D), F32), (row, BF16)],
            [x0, x1, x2, h, dq, dk, dv, da, o, w_attn, dx, gain_attn],
            scratch=[pltpu.VMEM(row, F32)] + [pltpu.VMEM(row, BF16)] * 4 + [dma(2), dma(2)],
            meet=2,
        )
        back_grad = lax.all_to_all(d_start, "dp", split_axis=0, concat_axis=0, tiled=True)
        output, grad_tokens = call(restore_body, "restore", [(row, BF16)] * 2, [pos, back_out, back_grad])

        def total(v):
            for axis, count in (("tensor", n_t), ("dp", n_dp)):
                bit = 1
                while bit < count:
                    v = v + lax.ppermute(v, axis, [(i, i ^ bit) for i in range(count)])
                    bit *= 2
            return v

        small_all = total(jnp.concatenate([small, gain_part], axis=0))
        gain_all = small_all[SPARE + 8]
        gw_attn, ff_sum = lax.optimization_barrier((gw_attn, ff_sum))
        attn_sum = lax.psum_scatter(gw_attn, "dp", scatter_dimension=0, tiled=True).reshape(d_here, 4, n_t, D // n_t)

        def share(j):
            return lax.dynamic_index_in_dim(attn_sum, t ^ j, 2, keepdims=False)

        attn_own = share(0).astype(F32)
        for j in range(1, n_t):
            attn_own = attn_own + swap(share(j), j).astype(F32)
    ff_own = ff_sum.reshape(d_here, EXPERTS, 3 * ff).astype(F32)
    return (
        output,
        grad_tokens,
        dres[0:12].T,
        attn_own[:, 0:3],
        attn_own[:, 3],
        ff_own[:, :, 0 : 2 * ff].reshape(d_here, EXPERTS, 2, ff),
        ff_own[:, :, 2 * ff :],
        gain_all,
        small_all[SPARE + 2],
        small_all[0:12].T,
        small_all[12:16].reshape(2, 2, D).transpose(0, 2, 1),
        small_all[SPARE : SPARE + 2],
    )


def solution(mesh):
    both, every = P(("dp", "tensor"), None), P()
    weights = (P("dp", None, "tensor"), P("dp", "tensor"), P("dp", None, None, "tensor"), P("dp", None, "tensor"))
    return jax.shard_map(
        body,
        mesh=mesh,
        in_specs=(both, both, P(("dp", "tensor")), P("dp", None), P("dp", None), both, *weights) + (every,) * 5,
        out_specs=(both, both, both, *weights) + (every,) * 5,
        check_vma=False,
    )
```

profile of v0, /device:TPU:0, one launch (start us, length us, event | category | flops | bytes accessed | tf_op | source)
XLA Modules:
  0.0 494.4 jit_solution(15656353778333729407)
XLA Ops:
  7.3 2.9 reshape.85
  10.2 0.7 maximum_bitcast_fusion.ws_ref
  10.9 1.6 pad_maximum_fusion
  12.5 3.5 deal.1
  16.0 55.0 %opening.1 = (bf16[8,64,768]{2,1,0:T(8,128)(2,1)}, bf16[8,64,768]{2,1,0:T(8,128)(2,1)}, bf16[8,96,3072]{2,1,0:T(8,128)(2,1)}, bf16[8,64,768]{2,1,0:T(8,128)(2,1)...) custom-call(s32[8]{0:T(128)} %bitcast.62, ...), custom_call_target="tpu_custom_call" | custom-call | tf_op jit(solution)/shard_map/opening/pallas_call | solution.py:63
  70.9 3.9 copy.28
  77.3 0.6 concatenate.17.refs_10_
  78.7 0.6 pad_maximum_fusion.2.refs_11_.wrc_ref
  79.3 123.2 %forward.1 = (bf16[1536,768]{1,0:T(8,128)(2,1)}, bf16[512,768]{1,0:T(8,128)(2,1)}, bf16[1536,768]{1,0:T(8,128)(2,1)}, bf16[1536,768]{1,0:T(8,128)(2,1)}, bf16[51...) custom-call(bf16[8,64,768]{2,1,0:T(8,128)(2,1)} %get-tuple-element.5, ...), custom_call_target="tpu_custom_call" | custom-call | tf_op jit(solution)/shard_map/forward/pallas_call | solution.py:63
  202.6 76.4 %experts.1 = (bf16[4,512,768]{2,1,0:T(8,128)(2,1)}, bf16[4,528,768]{2,1,0:T(8,128)(2,1)}, bf16[768,12288]{1,0:T(8,128)(2,1)}) custom-call(s32[32]{0:T(128)} %reshape_squeeze.3.cnt_ref, bf16[4,528,768]{2,1,0:T(8,128)(2,1)} %get-tuple-element.69.h_refs.hp_ref, bf16[4,512,768]{2,1,0:T(8,128)(2,1)} %bitcast.48, s32[4,8,512]{2,1,0:T(8,128)} %get-tuple-element.71.slot_ref, ...), custom_call_target="tpu_custom_call" | custom-call | tf_op jit(solution)/shard_map/experts/pallas_call | solution.py:1149
  279.0 114.8 %backward.1 = (f32[512,768]{1,0:T(8,128)}, bf16[512,768]{1,0:T(8,128)(2,1)}, f32[16,512]{1,0:T(8,128)}, f32[24,768]{1,0:T(8,128)}, bf16[512,768]{1,0:T(8,128)(2,...) custom-call(bf16[4,528,768]{2,1,0:T(8,128)(2,1)} %get-tuple-element.73.back_ref, ...), custom_call_target="tpu_custom_call" | custom-call | tf_op jit(solution)/shard_map/backward/pallas_call | solution.py:63
  393.8 73.0 %finish.1 = (bf16[512,768]{1,0:T(8,128)(2,1)}, bf16[512,768]{1,0:T(8,128)(2,1)}, f32[4,96,192]{2,1,0:T(8,128)}, f32[32,768]{1,0:T(8,128)}) custom-call(bf16[512,768]{1,0:T(8,128)(2,1)} %bitcast.44, bf16[512,768]{1,0:T(8,128)(2,1)} %bitcast.45, bf16[512,768]{1,0:T(8,128)(2,1)} %bitcast.46, bf16[1536,768]{1,0:T(8,128)(2,1)} %get-tuple-element.67.h_ref, ...), custom_call_target="tpu_custom_call" | custom-call | tf_op jit(solution)/shard_map/finish/pallas_call | solution.py:63
  466.8 1.3 slice.51
  468.1 0.7 slice.50
  468.9 0.6 reshape.98
  469.5 1.4 slice_reduce_fusion.1
  470.9 1.7 slice_bitcast_fusion
  472.6 0.7 pad_maximum_fusion.1
  473.9 1.4 slice_bitcast_fusion.4
  475.3 2.5 copy.29
  477.8 1.3 slice.53
  479.4 3.7 reshape.97
  483.1 2.1 copy.32
  485.2 2.1 copy.33
  (36 shorter events, 4.2 us)
Async XLA Ops:
  7.2 3.0 copy-start.2
  7.2 3.0 copy-start.1
  7.2 3.7 copy-start
  7.2 195.3 %all-gather.2.cloned.1.call-start = ((), (), s32[]{:S(2)}) async-start(), calls=%async_computation.1 | async-start | bytes 21233664 | tf_op jit(solution)/shard_map/all_gather | solution.py:1244
  74.8 0.7 copy-start.9
  74.8 1.3 copy-start.10
  74.8 1.8 copy-start.7
  74.8 1.9 copy-start.8
  74.8 2.5 copy-start.4
  74.9 3.1 copy-start.6
  74.9 3.8 copy-start.3
  74.9 400.4 %reduce-scatter.2.cloned.1.call-start = ((), (), s32[]{:S(2)}) async-start(), calls=%async_computation.2 | async-start | bytes 21233664 | tf_op jit(solution)/shard_map/reduce_scatter | solution.py:1266
  393.7 79.6 %copy-start.5 = (f32[16,512]{1,0:T(8,128)S(1)}, f32[16,512]{1,0:T(8,128)}, u32[]{:S(2)}) copy-start(f32[16,512]{1,0:T(8,128)} %get-tuple-element.96) | copy-start | bytes 98308
Sparse Core Ops, SparseCore 0:
  75.0 106.3 all-gather.1
  279.1 125.8 reduce-scatter.1
where the time goes:
time: 500 us; the launch traced here: 494 us
  Pallas kernels  446 us (89%)
  local copies, waits for them, and re-layouts  30.3 us (6%)
  between operations  14.5 us (3%)
    pallas_call x5, Pallas kernels, call(): pl.pallas_call(body, name=name, out_shape=[jax.ShapeDtypeStruct(*o) for o...  369 us
    pallas_call x1, Pallas kernels, experts_call(): pl.pallas_call(functools.partial(experts_body, ff, chunks), name='experts...  76.4 us
    unnamed x26, local copies, waits for them, and re-layouts  11.1 us
  transfers between devices with their start and end apart: 2, of which 0 were waited for; matrix products, arithmetic and copies ran while one was open for 2% of the time, Pallas kernels for 63%

commit v1 on v0

--- a/solution.py
+++ b/solution.py
@@ -270,7 +270,7 @@
     b0, b1 = first * m01, second * m11
     table = jnp.concatenate([a, b0, b1, jnp.zeros((125, rows), F32)], axis=0).T
     ac, b0c, b1c = table[:, 0:1], table[:, 1:2], table[:, 2:3]
-    v = v_ref[...]
+    v = jnp.concatenate([v_ref[...], jnp.zeros((6, D), F32)], axis=0)
     xl_ref[...] = x1_ref[...] + ac * hf + b0c * v[0:1] + b1c * v[1:2]
     dhl_ref[...] = ac * gf
     ones = jnp.ones((8, D), BF16)
@@ -801,9 +801,9 @@
 
 
 def finish_body(n_dp, size, x0_ref, x1_ref, x2_ref, h_ref, dq_ref, dk_ref, dv_ref, da_ref, o_ref, w_ref, dx_ref, gain_ref,
-                y_ref, small_ref, pos_ref,
-                yo_ref, go_ref, gw_ref, sum_ref,
-                d0_ref, d1_ref, d2_ref, ra_ref, rb_ref, out_ref, yr_ref, gr_ref, part_ref, r1_ref, r2_ref, r3_ref,
+                y_ref, small_ref,
+                yr_ref, gr_ref, gw_ref, sum_ref,
+                d0_ref, d1_ref, d2_ref, ra_ref, rb_ref, out_ref, part_ref, r1_ref, r2_ref, r3_ref,
                 zs_ref, zr_ref, cur_ref, got_ref,
                 sems_s, sems_r, sy, ry, sg, rg, s1, r1, s2, r2, s3, r3, sz, rz, sb, rb):
     rows = x0_ref.shape[0]
@@ -813,7 +813,6 @@
     block = 256
     net = Peers()
     d, t = net.d, net.t
-    place = pick(iota((rows, rows), 0) == pos_ref[...])
     about, along = around(d, n_dp), around(t, size)
     net.enter([{"dp": to} for _, to, _ in about] + [{"tensor": to} for _, to, _ in along])
 
@@ -969,7 +968,6 @@
     own(0)
     own(1)
     gathered(yr_ref, (sy, ry))
-    yo_ref[...] = mm(place, yr_ref[...].reshape(rows, D), TN).astype(BF16)
     quarter(2)
     quarter(3)
     small_in(2)
@@ -994,7 +992,6 @@
     for u in range(4):
         whole(u)
     gathered(gr_ref, (sg, rg))
-    go_ref[...] = mm(place, gr_ref[...].reshape(rows, D), TN).astype(BF16)
     line.leave()
     net.leave()
 
@@ -1223,7 +1220,6 @@
     window = LONGEST + 256
     res_t = jnp.concatenate([gate_residual.T, jnp.zeros((4, rows), F32)], axis=0)
     wrc = jnp.concatenate([w_router.T, w_const.transpose(0, 2, 1).reshape(4, D)], axis=0)
-    v8 = jnp.concatenate([v_const, jnp.zeros((6, D), F32)], axis=0)
     dma = lambda *shape: pltpu.SemaphoreType.DMA(shape)
     found = [(parts, BF16), (parts, BF16), ((3 * rows, 128), F32), ((3 * rows, 128), F32), ((1, rows), I32)]
     if fast:
@@ -1237,6 +1233,7 @@
             + [dma(2)] * 2 + [dma(2, 2)] * 2 + [dma(n_dp // 2)] * 2 + [dma(2)] * 2,
             meet=3,
         )
+        ff_shard = ff_shard.reshape(d_here, EXPERTS * 3 * ff)
         x0, ff_shard = lax.optimization_barrier((x0, ff_shard))
         given, more = [x0, g0, w_attn, x1, x2, cos, sin, start], []
     else:
@@ -1249,7 +1246,7 @@
         + [(ext, BF16), (row, BF16), (ext, BF16), (ext, BF16), (row, BF16), ((SPARE, rows), F32),
            (row, F32), (every_packed, BF16), ((n_t,) + parts, BF16), ((8, rows), F32), (row, F32), (row, F32), ((SPARE, rows), F32),
            ((8, D), F32)],
-        given + [gain_attn, gain_moe, res_t, wrc, routes_t, v8],
+        given + [gain_attn, gain_moe, res_t, wrc, routes_t, v_const],
         scalars=0 if fast else 1,
         scratch=[pltpu.VMEM((window, 256), F32), dma(2), dma(2)] + [dma(3)] * 8,
         meet=0,
@@ -1280,12 +1277,12 @@
         units = 4
         piece = (d_here, D)
         hops = 3 + (n_t - 1).bit_length()
-        output, grad_tokens, attn_parts, small_all = call(
+        back_out, back_grad, attn_parts, small_all = call(
             functools.partial(finish_body, n_dp, n_t),
             "finish",
-            [(row, BF16), (row, BF16), ((units, d_here, D // n_t), F32), ((SPARE + 16, D), F32)],
-            [x0, x1, x2, h, dq, dk, dv, da, o, w_attn, dx, gain_attn, result.reshape(n_dp, share, D), small, pos],
-            scratch=[pltpu.VMEM(row, F32)] + [pltpu.VMEM(row, BF16)] * 4 + [pltpu.VMEM((n_dp, share, D), BF16)] * 3
+            [(parts, BF16), (parts, BF16), ((units, d_here, D // n_t), F32), ((SPARE + 16, D), F32)],
+            [x0, x1, x2, h, dq, dk, dv, da, o, w_attn, dx, gain_attn, result.reshape(n_dp, share, D), small],
+            scratch=[pltpu.VMEM(row, F32)] + [pltpu.VMEM(row, BF16)] * 4 + [pltpu.VMEM((n_dp, share, D), BF16)]
             + [pltpu.VMEM((units, n_dp) + piece, BF16), pltpu.VMEM((units, 4) + piece, BF16), pltpu.VMEM((units, 2) + piece, BF16),
                pltpu.VMEM((units,) + piece, BF16), pltpu.VMEM((units, n_t, d_here, D // n_t), BF16),
                pltpu.VMEM((units, n_t - 1, d_here, D // n_t), BF16)]
@@ -1307,7 +1304,6 @@
             meet=2,
         )
         back_grad = lax.all_to_all(d_start, "dp", split_axis=0, concat_axis=0, tiled=True)
-        output, grad_tokens = call(restore_body, "restore", [(row, BF16)] * 2, [pos, back_out, back_grad])
 
         def total(v):
             for axis, count in (("tensor", n_t), ("dp", n_dp)):
@@ -1328,6 +1324,7 @@
         attn_own = share(0).astype(F32)
         for j in range(1, n_t):
             attn_own = attn_own + swap(share(j), j).astype(F32)
+    output, grad_tokens = call(restore_body, "restore", [(row, BF16)] * 2, [pos, back_out.reshape(row), back_grad.reshape(row)])
     ff_own = ff_sum.reshape(d_here, EXPERTS, 3 * ff).astype(F32)
     return (
         output,

time: 500 us -> 499 us (level)
  Pallas kernels: 446 us -> 456 us
  local copies, waits for them, and re-layouts: 30.3 us -> 22.5 us
    pallas_call x5 -> x6, Pallas kernels: 369 us -> 382 us  [call(): pl.pallas_call(body, name=name, out_shape=[jax.ShapeDtypeStruct(*o) for o...]
    unnamed x26 -> x24, local copies, waits for them, and re-layouts: 11.1 us -> 4.76 us
  transfers between devices with their start and end apart: 2 -> 2, of which waited for: 0 -> 0; matrix products, arithmetic and copies ran while one was open for 2% -> 2% of each run, Pallas kernels for 63% -> 65%
where the time goes in v1:
time: 499 us; the launch traced here: 496 us
  Pallas kernels  456 us (91%)
  local copies, waits for them, and re-layouts  22.5 us (5%)
  between operations  14.5 us (3%)
    pallas_call x6, Pallas kernels, call(): pl.pallas_call(body, name=name, out_shape=[jax.ShapeDtypeStruct(*o) for o...  382 us
    pallas_call x1, Pallas kernels, experts_call(): pl.pallas_call(functools.partial(experts_body, ff, chunks), name='experts...  74 us
  transfers between devices with their start and end apart: 2, of which 0 were waited for; matrix products, arithmetic and copies ran while one was open for 2% of the time, Pallas kernels for 65%

profile of v1, /device:TPU:0, one launch (start us, length us, event | category | flops | bytes accessed | tf_op | source)
XLA Modules:
  0.0 495.8 jit_solution(2104987613127893413)
XLA Ops:
  7.2 2.9 reshape.91
  10.3 2.2 copy.28
  12.5 0.7 maximum_bitcast_fusion.ws_ref
  13.3 3.5 deal.1
  16.8 55.0 %opening.1 = (bf16[8,64,768]{2,1,0:T(8,128)(2,1)}, bf16[8,64,768]{2,1,0:T(8,128)(2,1)}, bf16[8,96,3072]{2,1,0:T(8,128)(2,1)}, bf16[8,64,768]{2,1,0:T(8,128)(2,1)...) custom-call(s32[8]{0:T(128)} %bitcast.66, ...), custom_call_target="tpu_custom_call" | custom-call | tf_op jit(solution)/shard_map/opening/pallas_call | solution.py:63
  73.2 0.6 reshape_squeeze.3.cnt_ref
  73.8 0.6 concatenate.14.refs_10_
  74.4 0.6 pad_maximum_fusion.2.refs_11_.wrc_ref
  75.1 123.2 %forward.1 = (bf16[1536,768]{1,0:T(8,128)(2,1)}, bf16[512,768]{1,0:T(8,128)(2,1)}, bf16[1536,768]{1,0:T(8,128)(2,1)}, bf16[1536,768]{1,0:T(8,128)(2,1)}, bf16[51...) custom-call(bf16[8,64,768]{2,1,0:T(8,128)(2,1)} %get-tuple-element.6, ...), custom_call_target="tpu_custom_call" | custom-call | tf_op jit(solution)/shard_map/forward/pallas_call | solution.py:63
  198.3 74.0 %experts.1 = (bf16[4,512,768]{2,1,0:T(8,128)(2,1)}, bf16[4,528,768]{2,1,0:T(8,128)(2,1)}, bf16[768,12288]{1,0:T(8,128)(2,1)}) custom-call(s32[32]{0:T(128)} %reshape_squeeze.3.cnt_ref, bf16[4,528,768]{2,1,0:T(8,128)(2,1)} %get-tuple-element.72.h_refs.hp_ref, bf16[4,512,768]{2,1,0:T(8,128)(2,1)} %bitcast.50, s32[4,8,512]{2,1,0:T(8,128)} %get-tuple-element.74.slot_ref, ...), custom_call_target="tpu_custom_call" | custom-call | tf_op jit(solution)/shard_map/experts/pallas_call | solution.py:1146
  272.4 125.5 %backward.1 = (f32[512,768]{1,0:T(8,128)}, bf16[512,768]{1,0:T(8,128)(2,1)}, f32[16,512]{1,0:T(8,128)}, f32[24,768]{1,0:T(8,128)}, bf16[512,768]{1,0:T(8,128)(2,...) custom-call(bf16[4,528,768]{2,1,0:T(8,128)(2,1)} %get-tuple-element.76.back_ref, ...), custom_call_target="tpu_custom_call" | custom-call | tf_op jit(solution)/shard_map/backward/pallas_call | solution.py:63
  397.9 71.8 %finish.1 = (bf16[8,64,768]{2,1,0:T(8,128)(2,1)}, bf16[8,64,768]{2,1,0:T(8,128)(2,1)}, f32[4,96,192]{2,1,0:T(8,128)}, f32[32,768]{1,0:T(8,128)}) custom-call(bf16[512,768]{1,0:T(8,128)(2,1)} %bitcast.46, bf16[512,768]{1,0:T(8,128)(2,1)} %bitcast.47, bf16[512,768]{1,0:T(8,128)(2,1)} %bitcast.48, bf16[1536,768]{1,0:T(8,128)(2,1)} %get-tuple-element.70.h_ref, ...), custom_call_target="tpu_custom_call" | custom-call | tf_op jit(solution)/shard_map/finish/pallas_call | solution.py:63
  469.8 1.4 slice.51
  471.2 0.7 slice.50
  471.9 0.6 reshape.106
  472.5 3.3 restore.1
  475.8 1.4 slice_reduce_fusion.1
  477.2 1.7 slice_bitcast_fusion
  478.9 0.7 pad_maximum_fusion.1
  479.6 0.6 slice_bitcast_fusion.5
  480.2 0.6 slice_bitcast_fusion.4
  480.9 2.5 copy.29
  483.4 1.3 slice.53
  484.9 3.7 reshape.105
  (34 shorter events, 2.0 us)
Async XLA Ops:
  7.2 3.0 copy-start
  7.2 191.1 %all-gather.2.cloned.1.call-start = ((), (), s32[]{:S(2)}) async-start(), calls=%async_computation.1 | async-start | bytes 21233664 | tf_op jit(solution)/shard_map/all_gather | solution.py:1241
  10.3 2.2 copy-start.1
  10.3 2.2 copy-start.3
  16.7 55.1 %copy-start.9 = (f32[768]{0:T(1024)S(1)}, f32[768]{0:T(1024)}, u32[]{:S(2)}) copy-start(f32[768]{0:T(1024)} %param.26) | copy-start | bytes 9220
  16.7 55.7 %copy-start.10 = (f32[768]{0:T(1024)S(1)}, f32[768]{0:T(1024)}, u32[]{:S(2)}) copy-start(f32[768]{0:T(1024)} %param.27) | copy-start | bytes 9220
  16.7 56.3 %copy-start.8 = (f32[2,768,2]{1,2,0:T(2,128)S(1)}, f32[2,768,2]{1,2,0:T(2,128)}, u32[]{:S(2)}) copy-start(f32[2,768,2]{1,2,0:T(2,128)} %param.29) | copy-start | bytes 36868
  16.7 56.3 %copy-start.7 = (s32[4,8,128]{2,1,0:T(8,128)S(1)}, s32[4,8,128]{2,1,0:T(8,128)}, u32[]{:S(2)}) copy-start(s32[4,8,128]{2,1,0:T(8,128)} %get-tuple-element.71) | copy-start | bytes 49156
  16.7 57.1 %copy-start.5 = (f32[512,12]{0,1:T(8,128)S(1)}, f32[512,12]{0,1:T(8,128)}, u32[]{:S(2)}) copy-start(f32[512,12]{0,1:T(8,128)} %param.21) | copy-start | bytes 73732
  16.7 57.7 %copy-start.4 = (f32[768,12]{0,1:T(8,128)S(1)}, f32[768,12]{0,1:T(8,128)}, u32[]{:S(2)}) copy-start(f32[768,12]{0,1:T(8,128)} %param.28) | copy-start | bytes 110596
  71.8 409.1 %reduce-scatter.2.cloned.1.call-start = ((), (), s32[]{:S(2)}) async-start(), calls=%async_computation.2 | async-start | bytes 21233664 | tf_op jit(solution)/shard_map/reduce_scatter | solution.py:1263
  469.7 9.9 %copy-start.6 = (f32[16,512]{1,0:T(8,128)S(1)}, f32[16,512]{1,0:T(8,128)}, u32[]{:S(2)}) copy-start(f32[16,512]{1,0:T(8,128)} %get-tuple-element.100) | copy-start | bytes 98308
  469.7 10.5 %copy-start.2 = (f32[32,768]{1,0:T(8,128)S(1)}, f32[32,768]{1,0:T(8,128)}, u32[]{:S(2)}) copy-start(f32[32,768]{1,0:T(8,128)} %get-tuple-element.103) | copy-start | bytes 294916
Sparse Core Ops, SparseCore 0:
  71.9 106.3 all-gather.1
  272.5 125.8 reduce-scatter.1
